TPU v7x, 32 devices: a whole 2x2x4 slice. The times are simulated.
32 devices in a mesh: sub: 8 (over z, y), freq: 4 (over x, core).
Axes of the slice: x: 2, y: 2, z: 4, core: 2. Of those that a mesh axis runs over, the one named last changes fastest.
Arguments:
- freq_squared: float32 [16], P('freq'), may hold values from 0.05 to 1
- displacement: bfloat16 [1536, 2048], P('freq', 'sub'), may hold values from -6 to 6
- adjoint: bfloat16 [1536, 2048], P('freq', 'sub'), may hold values from -6 to 6
- incidence: int32 [24, 4], P('sub'), may hold values from 0 to 15, as said below
- block_count: int32 [24], P('sub'), may hold values from 1 to 4, as said below
- mode_count: int32 [24], P('sub'), may hold values from 1 to 128, as said below
- stiffness: bfloat16 [24, 512, 512], P('sub'), may hold values from -0.25 to 0.25
- mass_matrix: bfloat16 [24, 512, 512], P('sub'), may hold values from -0.25 to 0.25
- coupling: bfloat16 [24, 128, 512], P('sub'), may hold values from -0.25 to 0.25
- eigenvalues: float32 [24, 128], P('sub'), may hold values from 1.5 to 20
- flexibility: float32 [24, 512], P('sub'), may hold values from 0.2 to 1
Outputs:
- interface_residual: float32 [1536, 2048], P('freq', 'sub')
- eigen_gradient: float32 [24, 128], P('sub')
- coupling_gradient: float32 [24, 128, 512], P('sub', None, 'freq')
- flexibility_gradient: float32 [24, 512], P('sub')
Inputs may be any that keep to these rules, and one draw needn't show every extreme that they name: `incidence`: every slot, live or not, names a block owned by the index of sub that holds the substructure or one at most 1 indices away (block b is owned by index b // 2). The first substructure of every index of sub touches, in live slots, a block of the owner 1 indices below and one 1 above wherever such owners exist. A substructure may name one block in several slots. `block_count`: the first substructure of every index of sub has 4 live slots. Modes j >= mode_count[s] are absent. The first substructure of every index of sub keeps 128 modes.
All inputs are finite; a program needn't handle non-finite values.
Results may differ from a plain program's by a relative error of at most 0.0029.
Values may be sent and summed in bfloat16 or wider, within the bound.
A program may use at most 64 MiB of HBM per device.

v0:
```python
import functools

import jax
import jax.numpy as jnp
from jax import lax
from jax.experimental import pallas as pl
from jax.experimental.pallas import tpu as pltpu
from jax.sharding import PartitionSpec as P

MESH = pl.DeviceIdType.MESH
NT = (((1,), (1,)), ((), ()))
NN = (((1,), (0,)), ((), ()))
TN = (((0,), (0,)), ((), ()))


def dot(a, b, dims):
    return lax.dot_general(a, b, dims, preferred_element_type=jnp.float32)


def kernel(
    n_sub,
    n_freq,
    chunks,
    freq_hbm,
    inc_hbm,
    count_hbm,
    mode_hbm,
    eig_hbm,
    flex_hbm,
    adj_ref,
    dis_ref,
    stiff_hbm,
    mass_hbm,
    coup_hbm,
    out_ref,
    eig_out,
    cg_out_ref,
    flex_out,
    *scratch,
):
    windows = scratch[:chunks]
    (
        freq_ref,
        inc_ref,
        count_ref,
        mode_ref,
        eig_ref,
        flex_ref,
        stiff,
        mass,
        coup,
        resp,
        weights,
        picked,
        near_acc,
        far_out,
        far_in,
        near_out,
        near_in,
        pack,
        grad,
        grad_out,
        grad_in,
        own_sem,
        weight_sem,
        small_sem,
        near_send,
        near_recv,
        relay_send,
        relay_recv,
        far_send,
        far_recv,
        back_send,
        back_recv,
        pack_send,
        pack_recv,
        grad_send,
        grad_recv,
    ) = scratch[chunks:]
    sub_here, slots = inc_ref.shape
    columns, owned_cells = adj_ref.shape
    rows = columns // chunks
    kb = stiff.shape[1]
    block = kb // slots
    owned = owned_cells // block
    modes = coup.shape[1]
    part = kb // n_freq

    me = lax.axis_index("sub")
    fr = lax.axis_index("freq")
    odd = me % 2
    step = 2 - 4 * odd
    partner = me + 1 - 2 * odd
    target = me + step
    source = me - step
    has_target = (target >= 0) & (target < n_sub)
    has_source = (source >= 0) & (source < n_sub)
    target = jnp.clip(target, 0, n_sub - 1)
    source = jnp.clip(source, 0, n_sub - 1)

    weight_copies = [
        pltpu.make_async_copy(hbm, vmem, weight_sem.at[i])
        for i, (hbm, vmem) in enumerate(((coup_hbm, coup), (stiff_hbm, stiff), (mass_hbm, mass)))
    ]
    small_copies = [
        pltpu.make_async_copy(hbm, local, small_sem.at[i])
        for i, (hbm, local) in enumerate(
            (
                (freq_hbm, freq_ref),
                (inc_hbm, inc_ref),
                (count_hbm, count_ref),
                (mode_hbm, mode_ref),
                (eig_hbm, eig_ref),
                (flex_hbm, flex_ref),
            )
        )
    ]
    own_copies = [
        [
            pltpu.make_async_copy(
                ref.at[pl.ds(c * rows, rows), :], windows[c].at[0, t], own_sem.at[c, t]
            )
            for t, ref in enumerate((adj_ref, dis_ref))
        ]
        for c in range(chunks)
    ]

    def remote(src, dst, send, recv, sub, freq):
        return pltpu.make_async_remote_copy(
            src_ref=src,
            dst_ref=dst,
            send_sem=send,
            recv_sem=recv,
            device_id=(sub, freq),
            device_id_type=MESH,
        )

    near_copies = [
        [
            remote(
                ref.at[pl.ds(c * rows, rows), :],
                windows[c].at[1, t],
                near_send.at[c, t],
                near_recv.at[c, t],
                partner,
                fr,
            )
            for t, ref in enumerate((adj_ref, dis_ref))
        ]
        for c in range(chunks)
    ]
    relay_copies = [
        [
            remote(
                windows[c].at[1, t],
                windows[c].at[2, t],
                relay_send.at[c, t],
                relay_recv.at[c, t],
                target,
                fr,
            )
            for t in range(2)
        ]
        for c in range(chunks)
    ]
    far_copies = [
        remote(far_out.at[c], far_in.at[c], far_send.at[c], far_recv.at[c], source, fr)
        for c in range(chunks)
    ]
    back_copies = [
        remote(near_out.at[c], near_in.at[c], back_send.at[c], back_recv.at[c], partner, fr)
        for c in range(chunks)
    ]
    peers = [(fr + d) % n_freq for d in range(n_freq)]
    pack_copies = [
        remote(pack.at[0], pack.at[d], pack_send.at[d], pack_recv.at[d], me, peers[d])
        for d in range(1, n_freq)
    ]
    grad_copies = [
        [
            remote(
                grad_out.at[s, peers[d]],
                grad_in.at[s, d],
                grad_send.at[s, d],
                grad_recv.at[s, d],
                me,
                peers[d],
            )
            for d in range(1, n_freq)
        ]
        for s in range(sub_here)
    ]

    barrier = pltpu.get_barrier_semaphore()

    def greet(sub, freq):
        pl.semaphore_signal(barrier, inc=1, device_id=(sub, freq), device_id_type=MESH)

    greet(partner, fr)
    for d in range(1, n_freq):
        greet(me, peers[d])

    @pl.when(has_target)
    def _():
        greet(target, fr)

    @pl.when(has_source)
    def _():
        greet(source, fr)

    for copy in small_copies:
        copy.start()
    for copies in own_copies[:1]:
        for copy in copies:
            copy.start()
    for copy in weight_copies:
        copy.start()
    for copies in own_copies[1:]:
        for copy in copies:
            copy.start()

    @pl.when(jnp.logical_not(has_target))
    def _():
        far_in[...] = jnp.zeros_like(far_in)

    pack[0] = jnp.zeros(pack.shape[1:], pack.dtype)
    pl.semaphore_wait(
        barrier, n_freq + has_target.astype(jnp.int32) + has_source.astype(jnp.int32)
    )
    for copies in near_copies:
        for copy in copies:
            copy.start()

    def relay(c):
        for copy in near_copies[c]:
            copy.wait_recv()

        @pl.when(has_target)
        def _():
            for copy in relay_copies[c]:
                copy.start()

    owners = (me, partner, me - 1 + 2 * odd)

    def hits(s, k):
        live = k < count_ref[s]
        named = inc_ref[s, k]
        return [live & (named == owner * owned + inner) for owner in owners for inner in range(owned)]

    def compute(c):
        window = windows[c]
        for copy in own_copies[c]:
            copy.wait()

        @pl.when(has_source)
        def _():
            for copy in relay_copies[c]:
                copy.wait_recv()

        if c == 0:
            for copy in small_copies + weight_copies:
                copy.wait()
        w2 = freq_ref[c]
        w4 = w2 * w2
        base = c * 2 * rows

        def one(s, carry):
            a_parts, d_parts = [], []
            zero = jnp.zeros((rows, block), jnp.bfloat16)
            for k in range(slots):
                a_part, d_part = zero, zero
                for w, hit in enumerate(hits(s, k)):
                    place, inner = w // owned, w % owned
                    lane = pl.ds(inner * block, block)
                    a_part = jnp.where(hit, window[place, 0, :, lane], a_part)
                    d_part = jnp.where(hit, window[place, 1, :, lane], d_part)
                a_parts.append(a_part)
                d_parts.append(d_part)
            a = jnp.concatenate(a_parts, axis=1)
            d = jnp.concatenate(d_parts, axis=1)
            af = a.astype(jnp.float32)
            df = d.astype(jnp.float32)
            picked[s, pl.ds(base, rows), :] = d
            picked[s, pl.ds(base + rows, rows), :] = a
            pack[0, s, 0:1, :] += -w4 * jnp.sum(af * df, axis=0, keepdims=True)
            couple = coup[s]
            ma = dot(a, couple, NT)
            md = dot(d, couple, NT)
            inverse = 1.0 / (eig_ref[pl.ds(s, 1), :] - w2)
            mode_index = lax.broadcasted_iota(jnp.int32, (1, modes), 1)
            factor = jnp.where(mode_index < mode_ref[s], w4 * inverse, 0.0)
            wa = (factor * ma).astype(jnp.bfloat16)
            wd = (factor * md).astype(jnp.bfloat16)
            weights[s, pl.ds(base, rows), :] = wa
            weights[s, pl.ds(base + rows, rows), :] = wd
            pack[0, s, 1:2, 0:modes] += (factor * inverse) * jnp.sum(
                ma * md, axis=0, keepdims=True
            )
            resp[s] = (
                dot(a, stiff[s], NT)
                - w2 * dot(a, mass[s], NT)
                - dot(wa, couple, NN)
                - (w4 * flex_ref[pl.ds(s, 1), :]) * af
            )
            return carry

        lax.fori_loop(0, sub_here, one, 0)

        places = [
            (s, k, [jnp.where(hit, 1.0, 0.0).astype(jnp.float32) for hit in hits(s, k)])
            for s in range(sub_here)
            for k in range(slots)
        ]
        here = pl.ds(c * rows, rows)
        for place in (2, 1, 0):
            for inner in range(owned):
                total = None
                for s, k, gains in places:
                    term = gains[place * owned + inner] * resp[s, :, k * block : (k + 1) * block]
                    total = term if total is None else total + term
                lane = pl.ds(inner * block, block)
                if place == 0:
                    out_ref[here, lane] = total
                elif place == 1:
                    near_acc[c, :, lane] = total
                else:
                    far_out[c, :, lane] = total.astype(far_out.dtype)

            if place == 2:

                @pl.when(has_source)
                def _():
                    far_copies[c].start()

    def combine(c):
        @pl.when(has_target)
        def _():
            far_copies[c].wait_recv()

        near_out[c] = (near_acc[c] + far_in[c].astype(jnp.float32)).astype(near_out.dtype)
        back_copies[c].start()

    def finish(c):
        back_copies[c].wait_recv()
        out_ref[pl.ds(c * rows, rows), :] += near_in[c].astype(jnp.float32)

    relay(0)
    for c in range(chunks):
        if c + 1 < chunks:
            relay(c + 1)
        compute(c)
        if c >= 2:
            combine(c - 2)

    for copy in pack_copies:
        copy.start()

    for s in range(sub_here):
        value = -dot(weights[s], picked[s], TN)
        for j in range(n_freq):
            piece = value[:, j * part : (j + 1) * part]
            grad[s, j] = piece
            grad_out[s, j] = piece.astype(grad_out.dtype)
        for copy in grad_copies[s]:
            copy.start()
    for c in range(max(chunks - 2, 0), chunks):
        combine(c)
    for c in range(chunks - 1):
        finish(c)

    for copy in pack_copies:
        copy.wait_recv()
    total = None
    for i in range(n_freq):
        term = pack[(fr - i + n_freq) % n_freq]
        total = term if total is None else total + term
    for s in range(sub_here):
        flex_out[s : s + 1, :] = total[s, 0:1, :]
        eig_out[s : s + 1, :] = total[s, 1:2, 0:modes]
    finish(chunks - 1)
    for s in range(sub_here):
        value = grad[s, fr]
        for d in range(1, n_freq):
            grad_copies[s][d - 1].wait_recv()
            value = value + grad_in[s, d].astype(jnp.float32)
        cg_out_ref[s] = value

    for c in range(chunks):
        for copy in near_copies[c]:
            copy.wait_send()
        back_copies[c].wait_send()

    @pl.when(has_target)
    def _():
        for c in range(chunks):
            for copy in relay_copies[c]:
                copy.wait_send()

    @pl.when(has_source)
    def _():
        for c in range(chunks):
            far_copies[c].wait_send()

    for copy in pack_copies:
        copy.wait_send()
    for s in range(sub_here):
        for copy in grad_copies[s]:
            copy.wait_send()


def write_out(*refs):
    count = len(refs) // 2
    sems = refs[-1]
    copies = [
        pltpu.make_async_copy(refs[i], refs[count + i], sems.at[i]) for i in range(count)
    ]
    for copy in copies:
        copy.start()
    for copy in copies:
        copy.wait()


def shards(
    n_sub,
    n_freq,
    freq_squared,
    displacement,
    adjoint,
    incidence,
    block_count,
    mode_count,
    stiffness,
    mass_matrix,
    coupling,
    eigenvalues,
    flexibility,
):
    sub_here = incidence.shape[0]
    columns, owned_cells = displacement.shape
    chunks = freq_squared.shape[0]
    rows = columns // chunks
    kb = stiffness.shape[1]
    modes = coupling.shape[1]
    part = kb // n_freq
    bf16, f32 = jnp.bfloat16, jnp.float32
    vmem = pl.BlockSpec(memory_space=pltpu.VMEM)
    hbm = pl.BlockSpec(memory_space=pltpu.HBM)
    dma = pltpu.SemaphoreType.DMA
    slab = (chunks, rows, owned_cells)
    scratch = [pltpu.VMEM((3, 2, rows, owned_cells), bf16) for _ in range(chunks)] + [
        pltpu.SMEM(freq_squared.shape, f32),
        pltpu.SMEM(incidence.shape, jnp.int32),
        pltpu.SMEM(block_count.shape, jnp.int32),
        pltpu.SMEM(mode_count.shape, jnp.int32),
        pltpu.VMEM(eigenvalues.shape, f32),
        pltpu.VMEM(flexibility.shape, f32),
        pltpu.VMEM(stiffness.shape, bf16),
        pltpu.VMEM(mass_matrix.shape, bf16),
        pltpu.VMEM(coupling.shape, bf16),
        pltpu.VMEM((sub_here, rows, kb), f32),
        pltpu.VMEM((sub_here, 2 * columns, modes), bf16),
        pltpu.VMEM((sub_here, 2 * columns, kb), bf16),
        pltpu.VMEM(slab, f32),
        pltpu.VMEM(slab, bf16),
        pltpu.VMEM(slab, bf16),
        pltpu.VMEM(slab, bf16),
        pltpu.VMEM(slab, bf16),
        pltpu.VMEM((n_freq, sub_here, 8, kb), f32),
        pltpu.VMEM((sub_here, n_freq, modes, part), f32),
        pltpu.VMEM((sub_here, n_freq, modes, part), bf16),
        pltpu.VMEM((sub_here, n_freq, modes, part), bf16),
        dma((chunks, 2)),
        dma((3,)),
        dma((6,)),
        dma((chunks, 2)),
        dma((chunks, 2)),
        dma((chunks, 2)),
        dma((chunks, 2)),
        dma((chunks,)),
        dma((chunks,)),
        dma((chunks,)),
        dma((chunks,)),
        dma((n_freq,)),
        dma((n_freq,)),
        dma((sub_here, n_freq)),
        dma((sub_here, n_freq)),
    ]
    results = pl.pallas_call(
        functools.partial(kernel, n_sub, n_freq, chunks),
        out_shape=(
            jax.ShapeDtypeStruct((columns, owned_cells), f32),
            jax.ShapeDtypeStruct((sub_here, modes), f32),
            jax.ShapeDtypeStruct((sub_here, modes, part), f32),
            jax.ShapeDtypeStruct((sub_here, kb), f32),
        ),
        in_specs=[hbm] * 11,
        out_specs=(vmem,) * 4,
        scratch_shapes=scratch,
        compiler_params=pltpu.CompilerParams(
            collective_id=0, has_side_effects=True, vmem_limit_bytes=48 * 1024 * 1024
        ),
    )(
        *(
            pltpu.with_memory_space_constraint(x, pltpu.HBM)
            for x in (
                freq_squared,
                incidence,
                block_count,
                mode_count,
                eigenvalues,
                flexibility,
                adjoint,
                displacement,
                stiffness,
                mass_matrix,
                coupling,
            )
        )
    )
    return pl.pallas_call(
        write_out,
        out_shape=tuple(jax.ShapeDtypeStruct(x.shape, x.dtype) for x in results),
        in_specs=[vmem] * 4,
        out_specs=(pl.BlockSpec(memory_space=pltpu.HBM),) * 4,
        scratch_shapes=[dma((4,))],
        compiler_params=pltpu.CompilerParams(vmem_limit_bytes=4 * 1024 * 1024),
    )(*results)


def solution(mesh):
    in_specs = (
        P("freq"),
        P("freq", "sub"),
        P("freq", "sub"),
        P("sub", None),
        P("sub"),
        P("sub"),
        P("sub", None, None),
        P("sub", None, None),
        P("sub", None, None),
        P("sub", None),
        P("sub", None),
    )
    out_specs = (P("freq", "sub"), P("sub", None), P("sub", None, "freq"), P("sub", None))
    body = functools.partial(shards, mesh.shape["sub"], mesh.shape["freq"])
    return jax.shard_map(body, mesh=mesh, in_specs=in_specs, out_specs=out_specs, check_vma=False)
```

profile of v0, /device:TPU:0, one launch (start us, length us, event | category | flops | bytes accessed | tf_op | source)
XLA Modules:
  0.0 30.9 jit_solution(4125307584840178514)
XLA Ops:
  0.6 29.5 %shard_map.138 = (f32[384,256]{1,0:T(8,128)S(1)}, f32[3,128]{1,0:T(4,128)S(1)}, f32[3,128,128]{2,1,0:T(8,128)S(1)}, f32[3,512]{1,0:T(4,128)S(1)}) custom-call(f32[4]{0:T(128)} %freq_hbm.1, s32[3,4]{1,0:T(4,128)} %inc_hbm.1, s32[3]{0:T(128)} %count_hbm.1, s32[3]{0:T(128)} %mode_hbm.1, f32[3,128]{1,0:T(4,128)} %eig_hbm.1, f32[3,512]{1,0:T(4,128)} %flex_hbm.1, ...), custom_call_target="tpu_custom_call" | custom-call | tf_op jit(solution)/shard_map/pallas_call | solution.py:488
  30.1 0.8 %shard_map.139 = (f32[384,256]{1,0:T(8,128)}, f32[3,128]{1,0:T(4,128)}, f32[3,128,128]{2,1,0:T(8,128)}, f32[3,512]{1,0:T(4,128)}) custom-call(f32[384,256]{1,0:T(8,128)S(1)} %get-tuple-element.8.refs_0_, f32[3,128]{1,0:T(4,128)S(1)} %get-tuple-element.9.refs_1_, f32[3,128,128]{2,1,0:T(8,128)S(1)} %get-tuple-element.10.refs_2_, ...), custom_call_target="tpu_custom_call" | custom-call | tf_op jit(solution)/shard_map/pallas_call | solution.py:520
where the time goes:
time: 31.1 us; the launch traced here: 30.9 us
  Pallas kernels  30.3 us (97%)
  between operations  0.64 us (2%)
    pallas_call x1, Pallas kernels, shards(): pl.pallas_call(functools.partial(kernel, n_sub, n_freq, chunks), out_shap...  29.5 us
    pallas_call x1, Pallas kernels, shards(): pl.pallas_call(write_out, out_shape=tuple((jax.ShapeDtypeStruct(x.shape,...  0.85 us

commit v1 on v0

v1 whole, which is shorter than its diff:
```python
import functools

import jax
import jax.numpy as jnp
from jax import lax
from jax.experimental import pallas as pl
from jax.experimental.pallas import tpu as pltpu
from jax.sharding import PartitionSpec as P

MESH = pl.DeviceIdType.MESH
NT = (((1,), (1,)), ((), ()))
NN = (((1,), (0,)), ((), ()))
TN = (((0,), (0,)), ((), ()))


def dot(a, b, dims):
    return lax.dot_general(a, b, dims, preferred_element_type=jnp.float32)


def group_of(chunks):
    return 2 if chunks % 2 == 0 else 1


def pair_of(n_freq):
    return 2 if n_freq % 2 == 0 else 1


def fold(x):
    return jnp.sum(x.reshape(x.shape[0] // 8, 8, x.shape[1]), axis=0)


def kernel(
    n_sub,
    n_freq,
    chunks,
    freq_hbm,
    inc_hbm,
    count_hbm,
    mode_hbm,
    eig_hbm,
    flex_hbm,
    adj_hbm,
    dis_hbm,
    stiff_hbm,
    mass_hbm,
    coup_hbm,
    out_ref,
    eig_out,
    cg_out_ref,
    flex_out,
    *scratch,
):
    group = group_of(chunks)
    halves = chunks // group
    win_a = scratch[:halves]
    win_d = scratch[halves : halves + chunks]
    (
        freq_ref,
        inc_ref,
        count_ref,
        mode_ref,
        block_tab,
        order_tab,
        last_tab,
        keep_tab,
        eig_ref,
        flex_ref,
        stiff,
        mass,
        coup,
        resp,
        runs,
        modal,
        weight_a,
        near_acc,
        far_out,
        far_in,
        near_out,
        near_in,
        flex_acc,
        eig_acc,
        pack,
        grad,
        first_out,
        first_in,
        second_out,
        second_in,
        own_sem,
        weight_sem,
        small_sem,
        near_send,
        near_recv,
        relay_send,
        relay_recv,
        far_send,
        far_recv,
        back_send,
        back_recv,
        pack_send,
        pack_recv,
        first_send,
        first_recv,
        second_send,
        second_recv,
    ) = scratch[halves + chunks :]
    sub_here, slots = inc_ref.shape
    columns, owned_cells = adj_hbm.shape
    rows = columns // chunks
    kb = stiff.shape[1]
    block = kb // slots
    owned = owned_cells // block
    modes = coup.shape[1]
    part = kb // n_freq
    n_slots = sub_here * slots
    spare = 3 * owned

    me = lax.axis_index("sub")
    fr = lax.axis_index("freq")
    odd = me % 2
    step = 2 - 4 * odd
    partner = me + 1 - 2 * odd
    target = me + step
    source = me - step
    has_target = (target >= 0) & (target < n_sub)
    has_source = (source >= 0) & (source < n_sub)
    target = jnp.clip(target, 0, n_sub - 1)
    source = jnp.clip(source, 0, n_sub - 1)

    weight_copies = [
        pltpu.make_async_copy(hbm, vmem, weight_sem.at[i])
        for i, (hbm, vmem) in enumerate(((coup_hbm, coup), (stiff_hbm, stiff), (mass_hbm, mass)))
    ]
    small_copies = [
        pltpu.make_async_copy(hbm, local, small_sem.at[i])
        for i, (hbm, local) in enumerate(
            (
                (freq_hbm, freq_ref),
                (inc_hbm, inc_ref),
                (count_hbm, count_ref),
                (mode_hbm, mode_ref),
                (eig_hbm, eig_ref),
                (flex_hbm, flex_ref),
            )
        )
    ]

    def here(c):
        return pl.ds(c * rows, rows)

    def within(c):
        return pl.ds((c % group) * rows, rows)

    def slab(t, c, place):
        blocks = pl.ds(place * owned, owned)
        if t == 0:
            return win_a[c // group].at[blocks, within(c), :]
        return win_d[c].at[blocks]

    def cell(t, c, inner):
        if t == 0:
            return win_a[c // group].at[inner, within(c), :]
        return win_d[c].at[inner]

    def remote(src, dst, send, recv, sub, freq):
        return pltpu.make_async_remote_copy(
            src_ref=src,
            dst_ref=dst,
            send_sem=send,
            recv_sem=recv,
            device_id=(sub, freq),
            device_id_type=MESH,
        )

    own_copies = [
        [
            [
                pltpu.make_async_copy(
                    ref.at[here(c), pl.ds(inner * block, block)],
                    cell(t, c, inner),
                    own_sem.at[t, c, inner],
                )
                for inner in range(owned)
            ]
            for c in range(chunks)
        ]
        for t, ref in enumerate((adj_hbm, dis_hbm))
    ]
    near_copies = [
        [
            remote(
                slab(t, c, 0), slab(t, c, 1), near_send.at[t, c], near_recv.at[t, c], partner, fr
            )
            for c in range(chunks)
        ]
        for t in range(2)
    ]
    relay_copies = [
        [
            remote(
                slab(t, c, 1), slab(t, c, 2), relay_send.at[t, c], relay_recv.at[t, c], target, fr
            )
            for c in range(chunks)
        ]
        for t in range(2)
    ]
    far_copies = [
        remote(far_out.at[c], far_in.at[c], far_send.at[c], far_recv.at[c], source, fr)
        for c in range(chunks)
    ]
    back_copies = [
        remote(near_out.at[c], near_in.at[c], back_send.at[c], back_recv.at[c], partner, fr)
        for c in range(chunks)
    ]
    peers = [(fr + d) % n_freq for d in range(n_freq)]
    pack_copies = [
        remote(pack.at[0], pack.at[d], pack_send.at[d], pack_recv.at[d], me, peers[d])
        for d in range(1, n_freq)
    ]
    pair = pair_of(n_freq)
    teams = n_freq // pair
    team = fr // pair
    rank = fr % pair
    other = (rank + 1) % pair
    first_copies = [
        remote(
            first_out.at[s, other],
            first_in.at[s],
            first_send.at[s],
            first_recv.at[s],
            me,
            team * pair + other,
        )
        for s in range(sub_here)
    ]
    away = [(team + d) % teams for d in range(teams)]
    second_copies = [
        [
            remote(
                second_out.at[s, d],
                second_in.at[s, d],
                second_send.at[s, d],
                second_recv.at[s, d],
                me,
                away[d] * pair + rank,
            )
            for d in range(1, teams)
        ]
        for s in range(sub_here)
    ]

    barrier = pltpu.get_barrier_semaphore()

    def greet(sub, freq):
        pl.semaphore_signal(barrier, inc=1, device_id=(sub, freq), device_id_type=MESH)

    greet(partner, fr)
    for d in range(1, n_freq):
        greet(me, peers[d])

    @pl.when(has_target)
    def _():
        greet(target, fr)

    @pl.when(has_source)
    def _():
        greet(source, fr)

    for copies in own_copies[0] + own_copies[1]:
        for copy in copies:
            copy.start()
    for copy in small_copies + weight_copies:
        copy.start()

    @pl.when(jnp.logical_not(has_target))
    def _():
        far_in[...] = jnp.zeros_like(far_in)

    for ref in (*win_a, *win_d):
        ref[spare] = jnp.zeros(ref.shape[1:], ref.dtype)
    runs[n_slots] = jnp.zeros(runs.shape[1:], runs.dtype)
    flex_acc[...] = jnp.zeros_like(flex_acc)
    eig_acc[...] = jnp.zeros_like(eig_acc)

    with jax.named_scope("barrier"):
        pl.semaphore_wait(
            barrier, n_freq + has_target.astype(jnp.int32) + has_source.astype(jnp.int32)
        )
    with jax.named_scope("near"):
        for t in range(2):
            for c in range(chunks):
                for copy in own_copies[t][c]:
                    copy.wait()
                near_copies[t][c].start()

    def relay(t, c):
        with jax.named_scope(f"relay{t}{c}"):
            near_copies[t][c].wait_recv()

            @pl.when(has_target)
            def _():
                relay_copies[t][c].start()

    def relayed(t, c):
        with jax.named_scope(f"relayed{t}{c}"):

            @pl.when(has_source)
            def _():
                relay_copies[t][c].wait_recv()

    with jax.named_scope("small"):
        for copy in small_copies:
            copy.wait()

    one, none = jnp.int32(1), jnp.int32(0)
    keys = []
    for s in range(sub_here):
        for k in range(slots):
            named = inc_ref[s, k]
            live = k < count_ref[s]
            key = jnp.int32(spare)
            for w, owner in enumerate((me, partner, me - 1 + 2 * odd)):
                for inner in range(owned):
                    hit = live & (named == owner * owned + inner)
                    key = jnp.where(hit, jnp.int32(w * owned + inner), key)
            block_tab[s * slots + k] = key
            keys.append(key)

    def count(tests):
        total = none
        for test in tests:
            total = total + jnp.where(test, one, none)
        return total

    ranks = [
        count(
            [keys[j] <= keys[i] for j in range(i)]
            + [keys[j] < keys[i] for j in range(i + 1, n_slots)]
        )
        for i in range(n_slots)
    ]
    before = None
    for r in range(n_slots):
        index, key = none, none
        for i in range(n_slots):
            chosen = ranks[i] == r
            index = jnp.where(chosen, jnp.int32(i), index)
            key = jnp.where(chosen, keys[i], key)
        order_tab[r] = index
        if r:
            keep_tab[r] = jnp.where(key == before, jnp.float32(1), jnp.float32(0))
        before = key
    for b in range(3 * owned):
        hits = count([key == b for key in keys])
        upto = count([key <= b for key in keys])
        last_tab[b] = jnp.where(hits > 0, upto - 1, jnp.int32(n_slots))

    for c in range(chunks):
        relay(0, c)

    def gather(ref, s, where):
        return jnp.concatenate(
            [ref[block_tab[s * slots + k], where, :] for k in range(slots)],
            axis=1,
        )

    def scales(c, s):
        w2 = freq_ref[c]
        w4 = w2 * w2
        inverse = 1.0 / (eig_ref[pl.ds(s, 1), :] - w2)
        mode_index = lax.broadcasted_iota(jnp.int32, (1, modes), 1)
        factor = jnp.where(mode_index < mode_ref[s], w4 * inverse, 0.0)
        return w2, w4, inverse, factor

    tile = 2 * block if slots % 2 == 0 else block

    def respond(p, s):
        a = gather(win_a[p], s, pl.ds(0, group * rows))
        couple = coup[s]
        ma = dot(a, couple, NT)
        parts = []
        for i in range(group):
            c = p * group + i
            factor = scales(c, s)[3]
            piece = ma[i * rows : (i + 1) * rows]
            modal[s, here(c), :] = piece
            parts.append((-factor * piece).astype(jnp.bfloat16))
        wa = jnp.concatenate(parts, axis=0)
        weight_a[s, pl.ds(p * group * rows, group * rows), :] = wa
        for n in range(kb // tile):
            lanes = slice(n * tile, (n + 1) * tile)
            plain = dot(a, stiff[s, lanes, :], NT) + dot(wa, couple[:, lanes], NN)
            inert = dot(a, mass[s, lanes, :], NT)
            for i in range(group):
                c = p * group + i
                w2, w4 = scales(c, s)[:2]
                span = slice(i * rows, (i + 1) * rows)
                value = (
                    plain[span]
                    - w2 * inert[span]
                    - (w4 * flex_ref[s : s + 1, lanes]) * a[span, lanes].astype(jnp.float32)
                )
                for k in range(tile // block):
                    slot = s * slots + n * (tile // block) + k
                    resp[slot, within(c), :] = value[:, k * block : (k + 1) * block]

    def spread(c):
        with jax.named_scope(f"spread{c}"):
            total = None
            for r in range(n_slots):
                term = resp[order_tab[r], within(c), :]
                total = term if total is None else total * keep_tab[r] + term
                runs[r] = total
            for place in (2, 1, 0):
                for inner in range(owned):
                    value = runs[last_tab[place * owned + inner]]
                    lane = pl.ds(inner * block, block)
                    if place == 0:
                        out_ref[here(c), lane] = value
                    elif place == 1:
                        near_acc[c, :, lane] = value
                    else:
                        far_out[c, :, lane] = value.astype(far_out.dtype)
                if place == 2:

                    @pl.when(has_source)
                    def _():
                        far_copies[c].start()

    steps = halves * sub_here
    passed = 0
    for p in range(halves):
        for i in range(group):
            relayed(0, p * group + i)
        if p == 0:
            with jax.named_scope("weights"):
                for copy in weight_copies:
                    copy.wait()
        for s in range(sub_here):
            with jax.named_scope(f"respond{p}{s}"):
                respond(p, s)
            due = min(chunks, ((2 * (p * sub_here + s) + 3) * chunks) // (2 * steps))
            while passed < due:
                relay(1, passed)
                passed += 1
        for i in range(group):
            spread(p * group + i)
    while passed < chunks:
        relay(1, passed)
        passed += 1

    def modal_part(c, s):
        ref = win_d[c]
        w2, w4, inverse, factor = scales(c, s)
        d = gather(ref, s, pl.ds(0, rows))
        a = gather(win_a[c // group], s, within(c))
        md = dot(d, coup[s], NT)
        wd = (-factor * md).astype(jnp.bfloat16)
        eig_acc[s] += (factor * inverse) * fold(modal[s, here(c), :] * md)
        left = jnp.concatenate([weight_a[s, here(c), :], wd], axis=0)
        right = jnp.concatenate([d, a], axis=0)
        value = dot(left, right, TN)
        if c:
            value = value + grad[s]
        if c + 1 < chunks:
            grad[s] = value
            return
        grad[s] = value
        for j in range(n_freq):
            first_out[s, j % pair, j // pair] = value[:, j * part : (j + 1) * part].astype(
                first_out.dtype
            )
        if pair > 1:
            first_copies[s].start()

    def flex_part(c):
        w4 = freq_ref[c] * freq_ref[c]
        for place in range(3):
            for inner in range(owned):
                b = place * owned + inner
                a = win_a[c // group][b, within(c), :].astype(jnp.float32)
                d = win_d[c][b].astype(jnp.float32)
                flex_acc[b] += -w4 * fold(a * d)

    def combine(c):
        with jax.named_scope(f"combine{c}"):

            @pl.when(has_target)
            def _():
                far_copies[c].wait_recv()

            near_out[c] = (near_acc[c] + far_in[c].astype(jnp.float32)).astype(near_out.dtype)
            back_copies[c].start()

    def finish(c):
        with jax.named_scope(f"finish{c}"):
            back_copies[c].wait_recv()
            out_ref[here(c), :] += near_in[c].astype(jnp.float32)

    combined = 0
    for c in range(chunks):
        relayed(1, c)
        with jax.named_scope(f"modal{c}"):
            for s in range(sub_here):
                modal_part(c, s)
        with jax.named_scope(f"flex{c}"):
            flex_part(c)
        if 1 <= c < chunks - 1:
            combine(combined)
            combined += 1

    with jax.named_scope("pack"):
        wide = max(block, modes)
        pack[0] = jnp.zeros(pack.shape[1:], pack.dtype)
        for s in range(sub_here):
            base = s * (slots + 1)
            for k in range(slots):
                pack[0, base + k : base + k + 1, 0:block] = jnp.sum(
                    flex_acc[block_tab[s * slots + k]], axis=0, keepdims=True
                )
            pack[0, base + slots : base + slots + 1, 0:modes] = jnp.sum(
                eig_acc[s], axis=0, keepdims=True
            )
        for copy in pack_copies:
            copy.start()

    while combined < chunks:
        combine(combined)
        combined += 1

    for s in range(sub_here):
        with jax.named_scope(f"second{s}"):
            if pair > 1:
                first_copies[s].wait_recv()
            for d in range(1, teams):
                j = away[d]
                lane = pl.ds(pl.multiple_of((j * pair + rank) * part, part), part)
                value = grad[s, :, lane]
                if pair > 1:
                    value = value + first_in[s, j].astype(jnp.float32)
                second_out[s, d] = value.astype(second_out.dtype)
            for copy in second_copies[s]:
                copy.start()

    for c in range(chunks):
        finish(c)

    with jax.named_scope("packwait"):
        for copy in pack_copies:
            copy.wait_recv()
    total = None
    for i in range(n_freq):
        term = pack[(fr - i + n_freq) % n_freq]
        total = term if total is None else total + term
    for s in range(sub_here):
        base = s * (slots + 1)
        for k in range(slots):
            flex_out[s : s + 1, k * block : (k + 1) * block] = total[
                base + k : base + k + 1, 0:block
            ]
        eig_out[s : s + 1, :] = total[base + slots : base + slots + 1, 0:modes]
    for s in range(sub_here):
        with jax.named_scope(f"grad{s}"):
            lane = pl.ds(pl.multiple_of(fr * part, part), part)
            value = grad[s, :, lane]
            if pair > 1:
                value = value + first_in[s, team].astype(jnp.float32)
            for d in range(1, teams):
                second_copies[s][d - 1].wait_recv()
                value = value + second_in[s, d].astype(jnp.float32)
            cg_out_ref[s] = value

    with jax.named_scope("end"):
        for c in range(chunks):
            for t in range(2):
                near_copies[t][c].wait_send()
            back_copies[c].wait_send()

        @pl.when(has_target)
        def _():
            for c in range(chunks):
                for t in range(2):
                    relay_copies[t][c].wait_send()

        @pl.when(has_source)
        def _():
            for c in range(chunks):
                far_copies[c].wait_send()

        for copy in pack_copies:
            copy.wait_send()
        for s in range(sub_here):
            if pair > 1:
                first_copies[s].wait_send()
            for copy in second_copies[s]:
                copy.wait_send()


def write_out(*refs):
    count = len(refs) // 2
    sems = refs[-1]
    copies = [
        pltpu.make_async_copy(refs[i], refs[count + i], sems.at[i]) for i in range(count)
    ]
    for copy in copies:
        copy.start()
    for copy in copies:
        copy.wait()


def shards(
    n_sub,
    n_freq,
    freq_squared,
    displacement,
    adjoint,
    incidence,
    block_count,
    mode_count,
    stiffness,
    mass_matrix,
    coupling,
    eigenvalues,
    flexibility,
):
    sub_here, slots = incidence.shape
    columns, owned_cells = displacement.shape
    chunks = freq_squared.shape[0]
    rows = columns // chunks
    kb = stiffness.shape[1]
    block = kb // slots
    owned = owned_cells // block
    modes = coupling.shape[1]
    part = kb // n_freq
    group = group_of(chunks)
    pair = pair_of(n_freq)
    teams = n_freq // pair
    n_slots = sub_here * slots
    pack_rows = -(-(sub_here * (slots + 1)) // 8) * 8
    bf16, f32, i32 = jnp.bfloat16, jnp.float32, jnp.int32
    vmem = pl.BlockSpec(memory_space=pltpu.VMEM)
    hbm = pl.BlockSpec(memory_space=pltpu.HBM)
    dma = pltpu.SemaphoreType.DMA
    slab = (chunks, rows, owned_cells)
    scratch = (
        [
            pltpu.VMEM((3 * owned + 1, group * rows, block), bf16)
            for _ in range(chunks // group)
        ]
        + [pltpu.VMEM((3 * owned + 1, rows, block), bf16) for _ in range(chunks)]
        + [
            pltpu.SMEM(freq_squared.shape, f32),
            pltpu.SMEM(incidence.shape, i32),
            pltpu.SMEM(block_count.shape, i32),
            pltpu.SMEM(mode_count.shape, i32),
            pltpu.SMEM((n_slots,), i32),
            pltpu.SMEM((n_slots,), i32),
            pltpu.SMEM((3 * owned,), i32),
            pltpu.SMEM((n_slots,), f32),
            pltpu.VMEM(eigenvalues.shape, f32),
            pltpu.VMEM(flexibility.shape, f32),
            pltpu.VMEM(stiffness.shape, bf16),
            pltpu.VMEM(mass_matrix.shape, bf16),
            pltpu.VMEM(coupling.shape, bf16),
            pltpu.VMEM((n_slots, group * rows, block), f32),
            pltpu.VMEM((n_slots + 1, rows, block), f32),
            pltpu.VMEM((sub_here, columns, modes), f32),
            pltpu.VMEM((sub_here, columns, modes), bf16),
            pltpu.VMEM(slab, f32),
            pltpu.VMEM(slab, bf16),
            pltpu.VMEM(slab, bf16),
            pltpu.VMEM(slab, bf16),
            pltpu.VMEM(slab, bf16),
            pltpu.VMEM((3 * owned + 1, 8, block), f32),
            pltpu.VMEM((sub_here, 8, modes), f32),
            pltpu.VMEM((n_freq, pack_rows, max(block, modes)), f32),
            pltpu.VMEM((sub_here, modes, kb), f32),
            pltpu.VMEM((sub_here, pair, teams, modes, part), bf16),
            pltpu.VMEM((sub_here, teams, modes, part), bf16),
            pltpu.VMEM((sub_here, teams, modes, part), bf16),
            pltpu.VMEM((sub_here, teams, modes, part), bf16),
            dma((2, chunks, owned)),
            dma((3,)),
            dma((6,)),
            dma((2, chunks)),
            dma((2, chunks)),
            dma((2, chunks)),
            dma((2, chunks)),
            dma((chunks,)),
            dma((chunks,)),
            dma((chunks,)),
            dma((chunks,)),
            dma((n_freq,)),
            dma((n_freq,)),
            dma((sub_here,)),
            dma((sub_here,)),
            dma((sub_here, teams)),
            dma((sub_here, teams)),
        ]
    )
    results = pl.pallas_call(
        functools.partial(kernel, n_sub, n_freq, chunks),
        out_shape=(
            jax.ShapeDtypeStruct((columns, owned_cells), f32),
            jax.ShapeDtypeStruct((sub_here, modes), f32),
            jax.ShapeDtypeStruct((sub_here, modes, part), f32),
            jax.ShapeDtypeStruct((sub_here, kb), f32),
        ),
        in_specs=[hbm] * 11,
        out_specs=(vmem,) * 4,
        scratch_shapes=scratch,
        compiler_params=pltpu.CompilerParams(
            collective_id=0, has_side_effects=True, vmem_limit_bytes=48 * 1024 * 1024
        ),
    )(
        *(
            pltpu.with_memory_space_constraint(x, pltpu.HBM)
            for x in (
                freq_squared,
                incidence,
                block_count,
                mode_count,
                eigenvalues,
                flexibility,
                adjoint,
                displacement,
                stiffness,
                mass_matrix,
                coupling,
            )
        )
    )
    return pl.pallas_call(
        write_out,
        out_shape=tuple(jax.ShapeDtypeStruct(x.shape, x.dtype) for x in results),
        in_specs=[vmem] * 4,
        out_specs=(pl.BlockSpec(memory_space=pltpu.HBM),) * 4,
        scratch_shapes=[dma((4,))],
        compiler_params=pltpu.CompilerParams(vmem_limit_bytes=4 * 1024 * 1024),
    )(*results)


def solution(mesh):
    in_specs = (
        P("freq"),
        P("freq", "sub"),
        P("freq", "sub"),
        P("sub", None),
        P("sub"),
        P("sub"),
        P("sub", None, None),
        P("sub", None, None),
        P("sub", None, None),
        P("sub", None),
        P("sub", None),
    )
    out_specs = (P("freq", "sub"), P("sub", None), P("sub", None, "freq"), P("sub", None))
    body = functools.partial(shards, mesh.shape["sub"], mesh.shape["freq"])
    return jax.shard_map(body, mesh=mesh, in_specs=in_specs, out_specs=out_specs, check_vma=False)
```

time: 31.1 us -> 27 us (0.87)
  Pallas kernels: 30.3 us -> 26.2 us
    pallas_call x1, Pallas kernels: 29.5 us -> 25.3 us  [shards(): pl.pallas_call(functools.partial(kernel, n_sub, n_freq, chunks), out_shap...]
where the time goes in v1:
time: 27 us; the launch traced here: 26.8 us
  Pallas kernels  26.2 us (97%)
  between operations  0.64 us (2%)
    pallas_call x1, Pallas kernels, shards(): pl.pallas_call(functools.partial(kernel, n_sub, n_freq, chunks), out_shap...  25.3 us
    pallas_call x1, Pallas kernels, shards(): pl.pallas_call(write_out, out_shape=tuple((jax.ShapeDtypeStruct(x.shape,...  0.85 us

profile of v1, /device:TPU:0, one launch (start us, length us, event | category | flops | bytes accessed | tf_op | source)
XLA Modules:
  0.0 26.8 jit_solution(6008458375403153671)
XLA Ops:
  0.6 25.3 %shard_map.138 = (f32[384,256]{1,0:T(8,128)S(1)}, f32[3,128]{1,0:T(4,128)S(1)}, f32[3,128,128]{2,1,0:T(8,128)S(1)}, f32[3,512]{1,0:T(4,128)S(1)}) custom-call(f32[4]{0:T(128)} %freq_hbm.1, s32[3,4]{1,0:T(4,128)} %inc_hbm.1, s32[3]{0:T(128)} %count_hbm.1, s32[3]{0:T(128)} %mode_hbm.1, f32[3,128]{1,0:T(4,128)} %eig_hbm.1, f32[3,512]{1,0:T(4,128)} %flex_hbm.1, ...), custom_call_target="tpu_custom_call" | custom-call | tf_op jit(solution)/shard_map/pallas_call | solution.py:700
  26.0 0.8 %shard_map.139 = (f32[384,256]{1,0:T(8,128)}, f32[3,128]{1,0:T(4,128)}, f32[3,128,128]{2,1,0:T(8,128)}, f32[3,512]{1,0:T(4,128)}) custom-call(f32[384,256]{1,0:T(8,128)S(1)} %get-tuple-element.8.refs_0_, f32[3,128]{1,0:T(4,128)S(1)} %get-tuple-element.9.refs_1_, f32[3,128,128]{2,1,0:T(8,128)S(1)} %get-tuple-element.10.refs_2_, ...), custom_call_target="tpu_custom_call" | custom-call | tf_op jit(solution)/shard_map/pallas_call | solution.py:732

commit v2 on v1

--- a/solution.py
+++ b/solution.py
@@ -271,10 +271,6 @@
     for copy in small_copies + weight_copies:
         copy.start()
 
-    @pl.when(jnp.logical_not(has_target))
-    def _():
-        far_in[...] = jnp.zeros_like(far_in)
-
     for ref in (*win_a, *win_d):
         ref[spare] = jnp.zeros(ref.shape[1:], ref.dtype)
     runs[n_slots] = jnp.zeros(runs.shape[1:], runs.dtype)
@@ -285,12 +281,19 @@
         pl.semaphore_wait(
             barrier, n_freq + has_target.astype(jnp.int32) + has_source.astype(jnp.int32)
         )
-    with jax.named_scope("near"):
-        for t in range(2):
-            for c in range(chunks):
-                for copy in own_copies[t][c]:
-                    copy.wait()
-                near_copies[t][c].start()
+    def send(t):
+        for c in range(chunks):
+            for copy in own_copies[t][c]:
+                copy.wait()
+            near_copies[t][c].start()
+
+    leads = rank == 0
+    follows = rank != 0
+
+    @pl.when(leads)
+    def _():
+        send(0)
+        send(1)
 
     def relay(t, c):
         with jax.named_scope(f"relay{t}{c}"):
@@ -354,8 +357,19 @@
         upto = count([key <= b for key in keys])
         last_tab[b] = jnp.where(hits > 0, upto - 1, jnp.int32(n_slots))
 
+    if pair > 1:
+
+        @pl.when(follows)
+        def _():
+            send(0)
+
     for c in range(chunks):
         relay(0, c)
+        if c == chunks - 1 and pair > 1:
+
+            @pl.when(follows)
+            def _():
+                send(1)
 
     def gather(ref, s, where):
         return jnp.concatenate(
@@ -373,35 +387,42 @@
 
     tile = 2 * block if slots % 2 == 0 else block
 
-    def respond(p, s):
-        a = gather(win_a[p], s, pl.ds(0, group * rows))
-        couple = coup[s]
-        ma = dot(a, couple, NT)
-        parts = []
-        for i in range(group):
-            c = p * group + i
-            factor = scales(c, s)[3]
-            piece = ma[i * rows : (i + 1) * rows]
-            modal[s, here(c), :] = piece
-            parts.append((-factor * piece).astype(jnp.bfloat16))
-        wa = jnp.concatenate(parts, axis=0)
-        weight_a[s, pl.ds(p * group * rows, group * rows), :] = wa
-        for n in range(kb // tile):
-            lanes = slice(n * tile, (n + 1) * tile)
-            plain = dot(a, stiff[s, lanes, :], NT) + dot(wa, couple[:, lanes], NN)
-            inert = dot(a, mass[s, lanes, :], NT)
+    def respond(p):
+        firsts, weights = [], []
+        for s in range(sub_here):
+            a = gather(win_a[p], s, pl.ds(0, group * rows))
+            ma = dot(a, coup[s], NT)
+            parts = []
             for i in range(group):
                 c = p * group + i
-                w2, w4 = scales(c, s)[:2]
-                span = slice(i * rows, (i + 1) * rows)
-                value = (
-                    plain[span]
-                    - w2 * inert[span]
-                    - (w4 * flex_ref[s : s + 1, lanes]) * a[span, lanes].astype(jnp.float32)
-                )
-                for k in range(tile // block):
-                    slot = s * slots + n * (tile // block) + k
-                    resp[slot, within(c), :] = value[:, k * block : (k + 1) * block]
+                factor = scales(c, s)[3]
+                piece = ma[i * rows : (i + 1) * rows]
+                modal[s, here(c), :] = piece
+                parts.append((-factor * piece).astype(jnp.bfloat16))
+            wa = jnp.concatenate(parts, axis=0)
+            weight_a[s, pl.ds(p * group * rows, group * rows), :] = wa
+            firsts.append(a)
+            weights.append(wa)
+        for s in range(sub_here):
+            a, wa = firsts[s], weights[s]
+            if s == min(1, sub_here - 1) and p == halves - 1:
+                pass_on(2)
+            for n in range(kb // tile):
+                lanes = slice(n * tile, (n + 1) * tile)
+                plain = dot(a, stiff[s, lanes, :], NT) + dot(wa, coup[s, :, lanes], NN)
+                inert = dot(a, mass[s, lanes, :], NT)
+                for i in range(group):
+                    c = p * group + i
+                    w2, w4 = scales(c, s)[:2]
+                    span = slice(i * rows, (i + 1) * rows)
+                    value = (
+                        plain[span]
+                        - w2 * inert[span]
+                        - (w4 * flex_ref[s : s + 1, lanes]) * a[span, lanes].astype(jnp.float32)
+                    )
+                    for k in range(tile // block):
+                        slot = s * slots + n * (tile // block) + k
+                        resp[slot, within(c), :] = value[:, k * block : (k + 1) * block]
 
     def spread(c):
         with jax.named_scope(f"spread{c}"):
@@ -426,8 +447,33 @@
                     def _():
                         far_copies[c].start()
 
-    steps = halves * sub_here
-    passed = 0
+            @pl.when(jnp.logical_not(has_target))
+            def _():
+                near_out[c] = near_acc[c].astype(near_out.dtype)
+                back_copies[c].start()
+
+    def plan(c, stages):
+        return stages[c * len(stages) // chunks]
+
+    def pass_on(position):
+        lead = [c for c in range(chunks) if plan(c, (0, 0, 1, 1)) == position]
+        follow = [c for c in range(chunks) if plan(c, (1, 2, 2, 3)) == position]
+        if pair == 1 or lead == follow:
+            for c in lead:
+                relay(1, c)
+            return
+
+        @pl.when(leads)
+        def _():
+            for c in lead:
+                relay(1, c)
+
+        @pl.when(follows)
+        def _():
+            for c in follow:
+                relay(1, c)
+
+    pass_on(0)
     for p in range(halves):
         for i in range(group):
             relayed(0, p * group + i)
@@ -435,42 +481,37 @@
             with jax.named_scope("weights"):
                 for copy in weight_copies:
                     copy.wait()
-        for s in range(sub_here):
-            with jax.named_scope(f"respond{p}{s}"):
-                respond(p, s)
-            due = min(chunks, ((2 * (p * sub_here + s) + 3) * chunks) // (2 * steps))
-            while passed < due:
-                relay(1, passed)
-                passed += 1
+        with jax.named_scope(f"respond{p}"):
+            respond(p)
         for i in range(group):
             spread(p * group + i)
-    while passed < chunks:
-        relay(1, passed)
-        passed += 1
-
-    def modal_part(c, s):
-        ref = win_d[c]
-        w2, w4, inverse, factor = scales(c, s)
-        d = gather(ref, s, pl.ds(0, rows))
-        a = gather(win_a[c // group], s, within(c))
-        md = dot(d, coup[s], NT)
-        wd = (-factor * md).astype(jnp.bfloat16)
-        eig_acc[s] += (factor * inverse) * fold(modal[s, here(c), :] * md)
-        left = jnp.concatenate([weight_a[s, here(c), :], wd], axis=0)
-        right = jnp.concatenate([d, a], axis=0)
-        value = dot(left, right, TN)
-        if c:
-            value = value + grad[s]
-        if c + 1 < chunks:
+        if p == 0:
+            pass_on(1)
+    pass_on(3)
+    def modal_part(c):
+        lefts, rights = [], []
+        for s in range(sub_here):
+            w2, w4, inverse, factor = scales(c, s)
+            d = gather(win_d[c], s, pl.ds(0, rows))
+            a = gather(win_a[c // group], s, within(c))
+            md = dot(d, coup[s], NT)
+            wd = (-factor * md).astype(jnp.bfloat16)
+            eig_acc[s] += (factor * inverse) * fold(modal[s, here(c), :] * md)
+            lefts.append(jnp.concatenate([weight_a[s, here(c), :], wd], axis=0))
+            rights.append(jnp.concatenate([d, a], axis=0))
+        for s in range(sub_here):
+            value = dot(lefts[s], rights[s], TN)
+            if c:
+                value = value + grad[s]
             grad[s] = value
-            return
-        grad[s] = value
-        for j in range(n_freq):
-            first_out[s, j % pair, j // pair] = value[:, j * part : (j + 1) * part].astype(
-                first_out.dtype
-            )
-        if pair > 1:
-            first_copies[s].start()
+            if c + 1 == chunks and pair > 1:
+                for j in range(n_freq):
+                    first_out[s, j % pair, j // pair] = value[
+                        :, j * part : (j + 1) * part
+                    ].astype(first_out.dtype)
+        if c + 1 == chunks and pair > 1:
+            for copy in first_copies:
+                copy.start()
 
     def flex_part(c):
         w4 = freq_ref[c] * freq_ref[c]
@@ -487,9 +528,10 @@
             @pl.when(has_target)
             def _():
                 far_copies[c].wait_recv()
-
-            near_out[c] = (near_acc[c] + far_in[c].astype(jnp.float32)).astype(near_out.dtype)
-            back_copies[c].start()
+                near_out[c] = (near_acc[c] + far_in[c].astype(jnp.float32)).astype(
+                    near_out.dtype
+                )
+                back_copies[c].start()
 
     def finish(c):
         with jax.named_scope(f"finish{c}"):
@@ -500,11 +542,10 @@
     for c in range(chunks):
         relayed(1, c)
         with jax.named_scope(f"modal{c}"):
-            for s in range(sub_here):
-                modal_part(c, s)
+            modal_part(c)
         with jax.named_scope(f"flex{c}"):
             flex_part(c)
-        if 1 <= c < chunks - 1:
+        if c == chunks - 2:
             combine(combined)
             combined += 1
 

time: 27 us -> 25.8 us (0.956)
  Pallas kernels: 26.2 us -> 25 us
    pallas_call x1, Pallas kernels: 25.3 us -> 24.1 us  [shards(): pl.pallas_call(functools.partial(kernel, n_sub, n_freq, chunks), out_shap...]
where the time goes in v2:
time: 25.8 us; the launch traced here: 25.6 us
  Pallas kernels  25 us (97%)
  between operations  0.64 us (2%)
    pallas_call x1, Pallas kernels, shards(): pl.pallas_call(functools.partial(kernel, n_sub, n_freq, chunks), out_shap...  24.1 us
    pallas_call x1, Pallas kernels, shards(): pl.pallas_call(write_out, out_shape=tuple((jax.ShapeDtypeStruct(x.shape,...  0.85 us

profile of v2, /device:TPU:0, one launch (start us, length us, event | category | flops | bytes accessed | tf_op | source)
XLA Modules:
  0.0 25.6 jit_solution(13051617891716266280)
XLA Ops:
  0.6 24.1 %shard_map.138 = (f32[384,256]{1,0:T(8,128)S(1)}, f32[3,128]{1,0:T(4,128)S(1)}, f32[3,128,128]{2,1,0:T(8,128)S(1)}, f32[3,512]{1,0:T(4,128)S(1)}) custom-call(f32[4]{0:T(128)} %freq_hbm.1, s32[3,4]{1,0:T(4,128)} %inc_hbm.1, s32[3]{0:T(128)} %count_hbm.1, s32[3]{0:T(128)} %mode_hbm.1, f32[3,128]{1,0:T(4,128)} %eig_hbm.1, f32[3,512]{1,0:T(4,128)} %flex_hbm.1, ...), custom_call_target="tpu_custom_call" | custom-call | tf_op jit(solution)/shard_map/pallas_call | solution.py:741
  24.8 0.8 %shard_map.139 = (f32[384,256]{1,0:T(8,128)}, f32[3,128]{1,0:T(4,128)}, f32[3,128,128]{2,1,0:T(8,128)}, f32[3,512]{1,0:T(4,128)}) custom-call(f32[384,256]{1,0:T(8,128)S(1)} %get-tuple-element.8.refs_0_, f32[3,128]{1,0:T(4,128)S(1)} %get-tuple-element.9.refs_1_, f32[3,128,128]{2,1,0:T(8,128)S(1)} %get-tuple-element.10.refs_2_, ...), custom_call_target="tpu_custom_call" | custom-call | tf_op jit(solution)/shard_map/pallas_call | solution.py:773

commit v3 on v2

--- a/solution.py
+++ b/solution.py
@@ -488,6 +488,7 @@
         if p == 0:
             pass_on(1)
     pass_on(3)
+
     def modal_part(c):
         lefts, rights = [], []
         for s in range(sub_here):
@@ -522,10 +523,10 @@
                 d = win_d[c][b].astype(jnp.float32)
                 flex_acc[b] += -w4 * fold(a * d)
 
-    def combine(c):
+    def combine(c, when=True):
         with jax.named_scope(f"combine{c}"):
 
-            @pl.when(has_target)
+            @pl.when(has_target & when)
             def _():
                 far_copies[c].wait_recv()
                 near_out[c] = (near_acc[c] + far_in[c].astype(jnp.float32)).astype(
@@ -545,9 +546,14 @@
             modal_part(c)
         with jax.named_scope(f"flex{c}"):
             flex_part(c)
+        if c == min(group, chunks) - 1:
+            for i in range(group):
+                combine(i, odd == 1)
+            combined = group
         if c == chunks - 2:
-            combine(combined)
-            combined += 1
+            combine(0, odd == 0)
+    for i in range(1 if chunks > 1 else 0, group):
+        combine(i, odd == 0)
 
     with jax.named_scope("pack"):
         wide = max(block, modes)
@@ -564,9 +570,8 @@
         for copy in pack_copies:
             copy.start()
 
-    while combined < chunks:
-        combine(combined)
-        combined += 1
+    for c in range(combined, chunks - 1):
+        combine(c, odd == 1)
 
     for s in range(sub_here):
         with jax.named_scope(f"second{s}"):
@@ -581,6 +586,11 @@
                 second_out[s, d] = value.astype(second_out.dtype)
             for copy in second_copies[s]:
                 copy.start()
+
+    for c in range(combined, chunks - 1):
+        combine(c, odd == 0)
+    for c in range(max(combined, chunks - 1), chunks):
+        combine(c)
 
     for c in range(chunks):
         finish(c)

time: 25.8 us -> 25 us (0.969)
  the two profiles are of different devices: /device:TPU:0 before, /device:TPU:13 now
where the time goes in v3:
time: 25 us; the launch traced here: 24.8 us
  Pallas kernels  24.2 us (97%)
  between operations  0.64 us (3%)
    pallas_call x1, Pallas kernels, shards(): pl.pallas_call(functools.partial(kernel, n_sub, n_freq, chunks), out_shap...  23.3 us
    pallas_call x1, Pallas kernels, shards(): pl.pallas_call(write_out, out_shape=tuple((jax.ShapeDtypeStruct(x.shape,...  0.85 us

profile of v3, /device:TPU:13, one launch (start us, length us, event | category | flops | bytes accessed | tf_op | source)
XLA Modules:
  0.0 24.8 jit_solution(3061593434323507748)
XLA Ops:
  0.6 23.3 %shard_map.138 = (f32[384,256]{1,0:T(8,128)S(1)}, f32[3,128]{1,0:T(4,128)S(1)}, f32[3,128,128]{2,1,0:T(8,128)S(1)}, f32[3,512]{1,0:T(4,128)S(1)}) custom-call(f32[4]{0:T(128)} %freq_hbm.1, s32[3,4]{1,0:T(4,128)} %inc_hbm.1, s32[3]{0:T(128)} %count_hbm.1, s32[3]{0:T(128)} %mode_hbm.1, f32[3,128]{1,0:T(4,128)} %eig_hbm.1, f32[3,512]{1,0:T(4,128)} %flex_hbm.1, ...), custom_call_target="tpu_custom_call" | custom-call | tf_op jit(solution)/shard_map/pallas_call | solution.py:751
  24.0 0.8 %shard_map.139 = (f32[384,256]{1,0:T(8,128)}, f32[3,128]{1,0:T(4,128)}, f32[3,128,128]{2,1,0:T(8,128)}, f32[3,512]{1,0:T(4,128)}) custom-call(f32[384,256]{1,0:T(8,128)S(1)} %get-tuple-element.8.refs_0_, f32[3,128]{1,0:T(4,128)S(1)} %get-tuple-element.9.refs_1_, f32[3,128,128]{2,1,0:T(8,128)S(1)} %get-tuple-element.10.refs_2_, ...), custom_call_target="tpu_custom_call" | custom-call | tf_op jit(solution)/shard_map/pallas_call | solution.py:783

commit v4 on v3

--- a/solution.py
+++ b/solution.py
@@ -156,6 +156,17 @@
             return win_a[c // group].at[blocks, within(c), :]
         return win_d[c].at[blocks]
 
+    def lot(t, c):
+        return c // group if t == 0 else halves + c
+
+    def sent(place, send, recv, sub):
+        for p in range(halves):
+            whole = win_a[p].at[pl.ds(place * owned, owned)]
+            remote(whole, whole, send.at[p], recv.at[0, p * group], sub, fr).wait_send()
+        for c in range(chunks):
+            whole = slab(1, c, place)
+            remote(whole, whole, send.at[halves + c], recv.at[1, c], sub, fr).wait_send()
+
     def cell(t, c, inner):
         if t == 0:
             return win_a[c // group].at[inner, within(c), :]
@@ -177,7 +188,7 @@
                 pltpu.make_async_copy(
                     ref.at[here(c), pl.ds(inner * block, block)],
                     cell(t, c, inner),
-                    own_sem.at[t, c, inner],
+                    own_sem.at[t, c],
                 )
                 for inner in range(owned)
             ]
@@ -188,7 +199,7 @@
     near_copies = [
         [
             remote(
-                slab(t, c, 0), slab(t, c, 1), near_send.at[t, c], near_recv.at[t, c], partner, fr
+                slab(t, c, 0), slab(t, c, 1), near_send.at[lot(t, c)], near_recv.at[t, c], partner, fr
             )
             for c in range(chunks)
         ]
@@ -197,23 +208,23 @@
     relay_copies = [
         [
             remote(
-                slab(t, c, 1), slab(t, c, 2), relay_send.at[t, c], relay_recv.at[t, c], target, fr
+                slab(t, c, 1), slab(t, c, 2), relay_send.at[lot(t, c)], relay_recv.at[t, c], target, fr
             )
             for c in range(chunks)
         ]
         for t in range(2)
     ]
     far_copies = [
-        remote(far_out.at[c], far_in.at[c], far_send.at[c], far_recv.at[c], source, fr)
+        remote(far_out.at[c], far_in.at[c], far_send.at[0], far_recv.at[c], source, fr)
         for c in range(chunks)
     ]
     back_copies = [
-        remote(near_out.at[c], near_in.at[c], back_send.at[c], back_recv.at[c], partner, fr)
+        remote(near_out.at[c], near_in.at[c], back_send.at[0], back_recv.at[c], partner, fr)
         for c in range(chunks)
     ]
     peers = [(fr + d) % n_freq for d in range(n_freq)]
     pack_copies = [
-        remote(pack.at[0], pack.at[d], pack_send.at[d], pack_recv.at[d], me, peers[d])
+        remote(pack.at[0], pack.at[d], pack_send.at[0], pack_recv.at[d - 1], me, peers[d])
         for d in range(1, n_freq)
     ]
     pair = pair_of(n_freq)
@@ -225,7 +236,7 @@
         remote(
             first_out.at[s, other],
             first_in.at[s],
-            first_send.at[s],
+            first_send.at[0],
             first_recv.at[s],
             me,
             team * pair + other,
@@ -236,10 +247,10 @@
     second_copies = [
         [
             remote(
-                second_out.at[s, d],
-                second_in.at[s, d],
-                second_send.at[s, d],
-                second_recv.at[s, d],
+                second_out.at[s, d - 1],
+                second_in.at[s, d - 1],
+                second_send.at[0],
+                second_recv.at[s, d - 1],
                 me,
                 away[d] * pair + rank,
             )
@@ -283,8 +294,7 @@
         )
     def send(t):
         for c in range(chunks):
-            for copy in own_copies[t][c]:
-                copy.wait()
+            pltpu.make_async_copy(slab(t, c, 0), slab(t, c, 0), own_sem.at[t, c]).wait()
             near_copies[t][c].start()
 
     leads = rank == 0
@@ -583,7 +593,7 @@
                 value = grad[s, :, lane]
                 if pair > 1:
                     value = value + first_in[s, j].astype(jnp.float32)
-                second_out[s, d] = value.astype(second_out.dtype)
+                second_out[s, d - 1] = value.astype(second_out.dtype)
             for copy in second_copies[s]:
                 copy.start()
 
@@ -617,33 +627,42 @@
                 value = value + first_in[s, team].astype(jnp.float32)
             for d in range(1, teams):
                 second_copies[s][d - 1].wait_recv()
-                value = value + second_in[s, d].astype(jnp.float32)
+                value = value + second_in[s, d - 1].astype(jnp.float32)
             cg_out_ref[s] = value
 
     with jax.named_scope("end"):
-        for c in range(chunks):
-            for t in range(2):
-                near_copies[t][c].wait_send()
-            back_copies[c].wait_send()
+        sent(0, near_send, near_recv, partner)
+        remote(near_out, near_in, back_send.at[0], back_recv.at[0], partner, fr).wait_send()
 
         @pl.when(has_target)
         def _():
-            for c in range(chunks):
-                for t in range(2):
-                    relay_copies[t][c].wait_send()
+            sent(1, relay_send, relay_recv, target)
 
         @pl.when(has_source)
         def _():
-            for c in range(chunks):
-                far_copies[c].wait_send()
-
-        for copy in pack_copies:
-            copy.wait_send()
-        for s in range(sub_here):
-            if pair > 1:
-                first_copies[s].wait_send()
-            for copy in second_copies[s]:
-                copy.wait_send()
+            remote(far_out, far_in, far_send.at[0], far_recv.at[0], source, fr).wait_send()
+
+        if n_freq > 1:
+            whole = pack.at[pl.ds(1, n_freq - 1)]
+            remote(whole, whole, pack_send.at[0], pack_recv.at[0], me, peers[1]).wait_send()
+        if pair > 1:
+            remote(
+                first_out.at[pl.ds(0, sub_here), other],
+                first_in,
+                first_send.at[0],
+                first_recv.at[0],
+                me,
+                team * pair + other,
+            ).wait_send()
+        if teams > 1:
+            remote(
+                second_out,
+                second_in,
+                second_send.at[0],
+                second_recv.at[0, 0],
+                me,
+                away[1] * pair + rank,
+            ).wait_send()
 
 
 def write_out(*refs):
@@ -727,25 +746,25 @@
             pltpu.VMEM((sub_here, modes, kb), f32),
             pltpu.VMEM((sub_here, pair, teams, modes, part), bf16),
             pltpu.VMEM((sub_here, teams, modes, part), bf16),
-            pltpu.VMEM((sub_here, teams, modes, part), bf16),
-            pltpu.VMEM((sub_here, teams, modes, part), bf16),
-            dma((2, chunks, owned)),
+            pltpu.VMEM((sub_here, max(teams - 1, 1), modes, part), bf16),
+            pltpu.VMEM((sub_here, max(teams - 1, 1), modes, part), bf16),
+            dma((2, chunks)),
             dma((3,)),
             dma((6,)),
+            dma((chunks // group + chunks,)),
             dma((2, chunks)),
+            dma((chunks // group + chunks,)),
             dma((2, chunks)),
-            dma((2, chunks)),
-            dma((2, chunks)),
+            dma((1,)),
             dma((chunks,)),
+            dma((1,)),
             dma((chunks,)),
-            dma((chunks,)),
-            dma((chunks,)),
-            dma((n_freq,)),
-            dma((n_freq,)),
+            dma((1,)),
+            dma((max(n_freq - 1, 1),)),
+            dma((1,)),
             dma((sub_here,)),
-            dma((sub_here,)),
-            dma((sub_here, teams)),
-            dma((sub_here, teams)),
+            dma((1,)),
+            dma((sub_here, max(teams - 1, 1))),
         ]
     )
     results = pl.pallas_call(

time: 25 us -> 24.7 us (0.988)
  Pallas kernels: 24.2 us -> 23.9 us
    pallas_call x1, Pallas kernels: 23.3 us -> 23 us  [shards(): pl.pallas_call(functools.partial(kernel, n_sub, n_freq, chunks), out_shap...]
where the time goes in v4:
time: 24.7 us; the launch traced here: 24.5 us
  Pallas kernels  23.9 us (97%)
  between operations  0.64 us (3%)
    pallas_call x1, Pallas kernels, shards(): pl.pallas_call(functools.partial(kernel, n_sub, n_freq, chunks), out_shap...  23 us
    pallas_call x1, Pallas kernels, shards(): pl.pallas_call(write_out, out_shape=tuple((jax.ShapeDtypeStruct(x.shape,...  0.85 us

profile of v4, /device:TPU:13, one launch (start us, length us, event | category | flops | bytes accessed | tf_op | source)
XLA Modules:
  0.0 24.5 jit_solution(4555349383579236929)
XLA Ops:
  0.6 23.0 %shard_map.138 = (f32[384,256]{1,0:T(8,128)S(1)}, f32[3,128]{1,0:T(4,128)S(1)}, f32[3,128,128]{2,1,0:T(8,128)S(1)}, f32[3,512]{1,0:T(4,128)S(1)}) custom-call(f32[4]{0:T(128)} %freq_hbm.1, s32[3,4]{1,0:T(4,128)} %inc_hbm.1, s32[3]{0:T(128)} %count_hbm.1, s32[3]{0:T(128)} %mode_hbm.1, f32[3,128]{1,0:T(4,128)} %eig_hbm.1, f32[3,512]{1,0:T(4,128)} %flex_hbm.1, ...), custom_call_target="tpu_custom_call" | custom-call | tf_op jit(solution)/shard_map/pallas_call | solution.py:770
  23.7 0.8 %shard_map.139 = (f32[384,256]{1,0:T(8,128)}, f32[3,128]{1,0:T(4,128)}, f32[3,128,128]{2,1,0:T(8,128)}, f32[3,512]{1,0:T(4,128)}) custom-call(f32[384,256]{1,0:T(8,128)S(1)} %get-tuple-element.8.refs_0_, f32[3,128]{1,0:T(4,128)S(1)} %get-tuple-element.9.refs_1_, f32[3,128,128]{2,1,0:T(8,128)S(1)} %get-tuple-element.10.refs_2_, ...), custom_call_target="tpu_custom_call" | custom-call | tf_op jit(solution)/shard_map/pallas_call | solution.py:802
